TPU v7x, 32 devices: a whole 2x2x4 slice. The times are simulated.
32 devices in a mesh: region: 4 (over z), dom: 8 (over y, x, core).
Axes of the slice: x: 2, y: 2, z: 4, core: 2. Of those that a mesh axis runs over, the one named last changes fastest.
Arguments:
- fine_blocks: bfloat16 [1536, 7, 128, 128], P(('region', 'dom')), may hold values from -6 to 6
- interp: bfloat16 [1536, 8192], P(('region', 'dom')), may hold values from -0.5 to 0.5
- fine_cols: int32 [1536, 7], P(('region', 'dom')), may hold values from 0 to 1535, as said below
- fine_slot: int32 [1536, 7], P(('region', 'dom')), may hold values from 0 to 6
- fine_owner: int32 [1536, 1], P(('region', 'dom')), may hold values from 0 to 7; in each aligned block of 48 rows (0 to 47, 48 to 95, ...) at most 6 rows name the same one
- fine_place: int32 [1536], P(('region', 'dom')), may hold values from 0 to 23
- coarse_interp: bfloat16 [768, 2048], P(('region', 'dom')), may hold values from -0.75 to 0.75
- coarse_cols: int32 [768, 7], P(('region', 'dom')), may hold values from 0 to 767, as said below
- coarse_slot: int32 [768, 7], P(('region', 'dom')), may hold values from 0 to 6
- coarse_owner: int32 [768, 1], P(('region', 'dom')), may hold values from 0 to 7; in each aligned block of 24 rows (0 to 23, 24 to 47, ...) at most 3 rows name the same one
- coarse_place: int32 [768], P(('region', 'dom')), may hold values from 0 to 11
Outputs:
- coarse_blocks: bfloat16 [768, 7, 4096], P(('region', 'dom'))
- coarse2_blocks: bfloat16 [384, 7, 1024], P(('region', 'dom'))
Inputs may be any that keep to these rules, and one draw needn't show every extreme that they name: fine_cols[i, 0] = i; every other entry names a fine row held by the device of the same dom index in the same region or in an adjacent region. coarse_cols[q, 0] = q; every other entry names a coarse row of the same region or of an adjacent region. `fine_owner`: among the rows of one device, no owner is named more than 6 times, a bound that some block reaches. `coarse_owner`: among the rows of one device, no owner is named more than 3 times, a bound that some block reaches.
All inputs are finite; a program needn't handle non-finite values.
Results may differ from a plain program's by a relative error of at most 0.0065.
Values may be sent and summed in bfloat16 or wider, within the bound.
No kernel may reach another device: no remote copies, remote signals or barrier semaphores. Data moves between devices by JAX's collectives and lax.ppermute only.
A program may use at most 128 MiB of HBM per device.

v0:
```python
import jax
import jax.numpy as jnp
from jax import lax
from jax.sharding import PartitionSpec as P


def extended(cells, sides, width):
    for axis, dim in sides:
        count = lax.axis_size(axis)
        ends = count - 1
        head = lax.slice_in_dim(cells, 0, width, axis=dim)
        tail = lax.slice_in_dim(cells, cells.shape[dim] - width, cells.shape[dim], axis=dim)
        cells = jnp.concatenate(
            [
                lax.ppermute(tail, axis, [(i, (i + 1) % count) for i in range(ends)]),
                cells,
                lax.ppermute(head, axis, [((i + 1) % count, i) for i in range(ends)]),
            ],
            axis=dim,
        )
    return cells


def block_products(blocks, picked):
    return jnp.einsum("rkab,rkbc->rkac", blocks, picked, preferred_element_type=jnp.float32).astype(
        jnp.bfloat16
    )


def slot_table(slot, stencil):
    letters = jnp.arange(stencil, dtype=jnp.int32)
    return (slot[:, :, None] == letters[None, None, :]).astype(jnp.float32)


def restrict_terms(product, own_rows, choose):
    count = product.shape[0]
    stencil = product.shape[1]
    narrow = own_rows.shape[2]
    term = jnp.einsum("rac,rkad->rkcd", own_rows, product, preferred_element_type=jnp.float32)
    term = term.reshape(count, stencil, narrow * narrow)
    return jnp.einsum("rks,rkx->rsx", choose, term, precision=lax.Precision.HIGHEST)


def block_terms(blocks, picked, own_rows, slot):
    product = block_products(blocks, picked)
    return restrict_terms(product, own_rows, slot_table(slot, blocks.shape[1]))


def owner_positions(owner, parts, capacity):
    member = (owner[:, None] == jnp.arange(parts, dtype=jnp.int32)[None, :]).astype(jnp.int32)
    before = jnp.cumsum(member, axis=0) - member
    rank = jnp.sum(before * member, axis=1)
    return owner * capacity + rank


def place_into(values, position, slots):
    return jnp.zeros((slots,) + values.shape[1:], values.dtype).at[position].set(values)


def pack_owned(values, owner, place, parts, capacity, owned):
    position = owner_positions(owner, parts, capacity)
    buffer = place_into(values, position, parts * capacity)
    labels = (place[:, None] == jnp.arange(owned, dtype=jnp.int32)[None, :]).astype(jnp.float32)
    marks = place_into(labels, position, parts * capacity)
    return (buffer, marks)


def local(
    fine_blocks,
    interp,
    fine_cols,
    fine_slot,
    fine_owner,
    fine_place,
    coarse_interp,
    coarse_cols,
    coarse_slot,
    coarse_owner,
    coarse_place,
):
    rows = fine_blocks.shape[0]
    stencil = fine_blocks.shape[1]
    width = fine_blocks.shape[2]
    narrow = interp.shape[1] // width
    narrow2 = coarse_interp.shape[1] // narrow
    parts = lax.axis_size("dom")
    region = lax.axis_index("region")
    owned = rows // 2
    owned2 = owned // 2
    capacity = max(2, rows // 8)
    capacity2 = max(2, owned // 8)
    nearby_rows = extended(interp, (("region", 0),), rows)
    span = parts * rows
    index = (fine_cols // span - region + 1) * rows + fine_cols % rows
    picked = nearby_rows[index].reshape(rows, stencil, width, narrow)
    own_rows = interp.reshape(rows, width, narrow)
    slotted = block_terms(fine_blocks, picked, own_rows, fine_slot)
    sent, marks = pack_owned(slotted, fine_owner[:, 0], fine_place, parts, capacity, owned)
    arrived, labels = (
        lax.all_to_all(sent, "dom", split_axis=0, concat_axis=0, tiled=True),
        lax.all_to_all(marks, "dom", split_axis=0, concat_axis=0, tiled=True),
    )
    coarse_sum = jnp.einsum("rc,rkx->ckx", labels, arrived, precision=lax.Precision.HIGHEST)
    coarse_blocks = coarse_sum.astype(jnp.bfloat16)
    span2 = parts * owned
    flat = coarse_interp.shape[1]
    widened = extended(coarse_interp, (("region", 0),), owned)
    stacked = widened.reshape(3, owned, flat)
    collected = lax.all_gather(stacked, "dom", axis=1, tiled=True)
    table = collected.reshape(3 * span2, flat)
    index2 = (coarse_cols // span2 - region + 1) * span2 + coarse_cols % span2
    picked2 = table[index2].reshape(owned, stencil, narrow, narrow2)
    square = coarse_blocks.reshape(owned, stencil, narrow, narrow)
    own_coarse = coarse_interp.reshape(owned, narrow, narrow2)
    slotted2 = block_terms(square, picked2, own_coarse, coarse_slot)
    sent2, marks2 = pack_owned(slotted2, coarse_owner[:, 0], coarse_place, parts, capacity2, owned2)
    arrived2, labels2 = (
        lax.all_to_all(sent2, "dom", split_axis=0, concat_axis=0, tiled=True),
        lax.all_to_all(marks2, "dom", split_axis=0, concat_axis=0, tiled=True),
    )
    second_sum = jnp.einsum("rc,rkx->ckx", labels2, arrived2, precision=lax.Precision.HIGHEST)
    return (coarse_blocks, second_sum.astype(jnp.bfloat16))


def solution(mesh):
    in_specs = (
        P(("region", "dom"), None, None, None),
        P(("region", "dom"), None),
        P(("region", "dom"), None),
        P(("region", "dom"), None),
        P(("region", "dom"), None),
        P(("region", "dom")),
        P(("region", "dom"), None),
        P(("region", "dom"), None),
        P(("region", "dom"), None),
        P(("region", "dom"), None),
        P(("region", "dom")),
    )
    out_specs = (P(("region", "dom"), None, None), P(("region", "dom"), None, None))
    return jax.shard_map(local, mesh=mesh, in_specs=in_specs, out_specs=out_specs, check_vma=False)
```

profile of v0, /device:TPU:0, one launch (start us, length us, event | category | flops | bytes accessed | tf_op | source)
XLA Modules:
  0.0 265.8 jit_solution(9862358425277935994)
XLA Ops:
  7.2 5.0 %collective-permute-start = (bf16[48,8192]{1,0:T(8,128)(2,1)}, bf16[48,8192]{1,0:T(8,128)(2,1)S(1)}, u32[]{:S(2)}, u32[]{:S(2)}) collective-permute-start(bf16[48,8192]{1,0:T(8,128)(2,1)} %param.12), channel_id=1, source_target_pairs={{0,8},{8,16},{16,24},{1,9},{9,17},{17,25},{2,10},{10,18},{18,26},{... | collective-permute-start | bytes 2359304 | tf_op jit(solution)/shard_map/ppermute | solution.py:15
  12.2 1.3 collective-permute-start.1
  17.4 3.7 %all-to-all-start = ((f32[8,1,144]{2,1,0:T(1,128)}), f32[8,1,144]{2,1,0:T(1,128)S(1)}, u32[]{:S(2)}, u32[]{:S(2)}) async-start(f32[8,1,144]{2,1,0:T(1,128)} %reshape.114), calls=%async_computation | async-start | bytes 16384 | tf_op jit(solution)/shard_map/all_to_all | solution.py:101
  21.1 3.4 %reshape.42 = bf16[48,128,64]{2,1,0:T(8,128)(2,1)} reshape(bf16[48,8192]{1,0:T(8,128)(2,1)} %param.12) | data formatting | bytes 1572864 | tf_op jit(solution)/shard_map/reshape | solution.py:96
  26.2 3.0 %collective-permute-done = bf16[48,8192]{1,0:T(8,128)(2,1)S(1)} collective-permute-done((bf16[48,8192]{1,0:T(8,128)(2,1)}, bf16[48,8192]{1,0:T(8,128)(2,1)S(1)}, u32[]{:S(2)}, u32[]{:S(2)}) %collective-permute-start) | collective-permute-done | bytes 786464 | tf_op jit(solution)/shard_map/ppermute | solution.py:15
  29.2 4.2 %collective-permute-done.1 = bf16[48,8192]{1,0:T(8,128)(2,1)} collective-permute-done((bf16[48,8192]{1,0:T(8,128)(2,1)}, bf16[48,8192]{1,0:T(8,128)(2,1)}, u32[]{:S(2)}, u32[]{:S(2)}) %collective-permute-start.1) | collective-permute-done | bytes 786464 | tf_op jit(solution)/shard_map/ppermute | solution.py:17
  33.4 1.5 pad_maximum_fusion
  34.9 6.9 %gather_fusion = bf16[336,8192]{1,0:T(8,128)(2,1)} fusion(bf16[144,8192]{1,0:T(8,128)(2,1)S(1)} %pad_maximum_fusion, s32[1024]{0:T(1024)S(1)} %pad_clamp_fusion.1), kind=kCustom, calls=%fused_computation | custom fusion | bytes 11011392 | tf_op jit(solution)/shard_map/gather | solution.py:95
  41.8 16.0 %reshape.41 = bf16[48,7,128,64]{3,2,1,0:T(8,128)(2,1)} reshape(bf16[336,8192]{1,0:T(8,128)(2,1)} %gather_fusion) | data formatting | bytes 11010048 | tf_op jit(solution)/shard_map/reshape | solution.py:95
  57.9 16.6 %fusion.10 = f32[48,7,64,64]{2,3,1,0:T(8,128)} fusion(bf16[48,7,128,64]{3,2,1,0:T(8,128)(2,1)} %reshape.41, bf16[48,7,128,128]{3,2,1,0:T(8,128)(2,1)} %param.11, bf16[48,128,64]{2,1,0:T(8,128)(2,1)S(1)} %copy-done), kind=kOutput, calls=%fused_computation.13 | convolution fusion | flops 1059717120 | bytes 22806528 | tf_op jit(solution)/shard_map/rac,rkad->rkcd/dot_general | solution.py:39
  74.4 12.2 %copy.58 = f32[48,7,64,64]{3,2,1,0:T(8,128)} copy(f32[48,7,64,64]{2,3,1,0:T(8,128)} %fusion.10) | data formatting | bytes 11010048 | tf_op jit(solution)/shard_map/reshape | solution.py:40
  86.6 10.3 %reshape.108 = f32[48,7,4096]{2,1,0:T(8,128)} reshape(f32[48,7,64,64]{3,2,1,0:T(8,128)} %copy.58) | data formatting | bytes 11010048 | tf_op jit(solution)/shard_map/reshape | solution.py:40
  96.9 8.4 %fusion.23 = f32[48,7,4096]{2,1,0:T(8,128)} fusion(f32[48,7,4096]{2,1,0:T(8,128)} %reshape.108, s32[48,7]{1,0:T(8,128)S(1)} %copy.31), kind=kOutput, calls=%fused_computation.25 | convolution fusion | flops 115607856 | bytes 11011392 | tf_op jit(solution)/shard_map/rks,rkx->rsx/dot_general | solution.py:41
  105.3 3.4 %broadcast_in_dim.13 = f32[48,7,4096]{2,1,0:T(8,128)} broadcast(f32[]{:T(128)} %constant.30.clone.1), dimensions={} | broadcast | bytes 5505028 | tf_op jit(solution)/shard_map/broadcast_in_dim | solution.py:57
  108.7 12.3 %scatter_fusion = f32[48,7,4096]{2,1,0:T(8,128)} fusion(f32[48,7,4096]{2,1,0:T(8,128)} %broadcast_in_dim.13, s32[48]{0:T(128)S(1)} %fusion.49, f32[48,7,4096]{2,1,0:T(8,128)} %fusion.23), kind=kCustom, calls=%fused_computation.3 | custom fusion | bytes 16515264 | tf_op jit(solution)/shard_map/scatter | solution.py:57
  121.0 4.9 %all-to-all-start.1 = ((f32[48,7,4096]{2,1,0:T(8,128)}), f32[48,7,4096]{2,1,0:T(8,128)}, u32[]{:S(2)}, u32[]{:S(2)}) async-start(f32[48,7,4096]{2,1,0:T(8,128)} %scatter_fusion), calls=%async_computation.1 | async-start | bytes 12582912 | tf_op jit(solution)/shard_map/all_to_all | solution.py:100
  126.0 3.4 %collective-permute-start.2 = (bf16[24,2048]{1,0:T(8,128)(2,1)S(1)}, bf16[24,2048]{1,0:T(8,128)(2,1)S(1)}, u32[]{:S(2)}, u32[]{:S(2)}) collective-permute-start(bf16[24,2048]{1,0:T(8,128)(2,1)S(1)} %copy-done.2), channel_id=1, source_target_pairs={{0,8},{8,16},{16,24},{1,9},{9,17},{17,25},{2,10},{10,18},{18,26},{... | collective-permute-start | bytes 294920 | tf_op jit(solution)/shard_map/ppermute | solution.py:15
  129.4 1.5 collective-permute-start.3
  132.0 4.1 %collective-permute-done.3 = bf16[24,2048]{1,0:T(8,128)(2,1)S(1)} collective-permute-done((bf16[24,2048]{1,0:T(8,128)(2,1)S(1)}, bf16[24,2048]{1,0:T(8,128)(2,1)S(1)}, u32[]{:S(2)}, u32[]{:S(2)}) %collective-permute-start.3) | collective-permute-done | bytes 98336 | tf_op jit(solution)/shard_map/ppermute | solution.py:17
  141.8 48.3 %all-gather.2.cloned.1.call-done = bf16[3,192,2048]{2,1,0:T(8,128)(2,1)} async-done(((bf16[3,24,2048]{2,1,0:T(8,128)(2,1)}), bf16[3,192,2048]{2,1,0:T(8,128)(2,1)}) %all-gather.2.cloned.1.call-update) | async-done | bytes 2359312 | tf_op jit(solution)/shard_map/all_gather | solution.py:109
  190.1 3.7 %gather_fusion.1 = bf16[168,2048]{1,0:T(8,128)(2,1)S(1)} fusion(bf16[576,2048]{1,0:T(8,128)(2,1)} %bitcast.52, s32[1024]{0:T(1024)S(1)} %pad_clamp_fusion), kind=kCustom, calls=%fused_computation.1 | custom fusion | bytes 1376928 | tf_op jit(solution)/shard_map/gather | solution.py:112
  193.8 2.0 reshape.47
  195.8 11.2 %all-to-all-done.1 = f32[48,7,4096]{2,1,0:T(8,128)} async-done(((f32[48,7,4096]{2,1,0:T(8,128)}), f32[48,7,4096]{2,1,0:T(8,128)}, u32[]{:S(2)}, u32[]{:S(2)}) %all-to-all-start.1) | async-done | bytes 5505056 | tf_op jit(solution)/shard_map/all_to_all | solution.py:100
  207.0 3.3 %all-to-all-start.2 = ((f32[8,3,12]{2,1,0:T(4,128)}), f32[8,3,12]{2,1,0:T(4,128)S(1)}, u32[]{:S(2)}, u32[]{:S(2)}) async-start(f32[8,3,12]{2,1,0:T(4,128)} %all_to_all.26), calls=%async_computation.2 | async-start | bytes 32768 | tf_op jit(solution)/shard_map/all_to_all | solution.py:119
  210.3 9.4 %fusion.7 = bf16[24,7,4096]{2,0,1:T(8,128)(2,1)} fusion(f32[48,7,4096]{2,1,0:T(8,128)} %all-to-all-done.1, f32[48,24]{1,0:T(8,128)S(1)} %all_to_all.24), kind=kOutput, calls=%fused_computation.12 | convolution fusion | flops 397049856 | bytes 6885888 | tf_op jit(solution)/shard_map/rc,rkx->ckx/dot_general | solution.py:103
  219.7 5.0 %reshape.44 = bf16[24,7,64,64]{3,2,0,1:T(8,128)(2,1)} reshape(bf16[24,7,4096]{2,0,1:T(8,128)(2,1)} %fusion.7) | data formatting | bytes 2752512 | tf_op jit(solution)/shard_map/reshape | solution.py:113
  224.7 5.3 %convolution_bitcast_fusion = f32[24,7,32,32]{2,3,1,0:T(8,128)} fusion(bf16[24,7,64,32]{3,2,1,0:T(8,128)(2,1)S(1)} %reshape.47, bf16[24,7,64,64]{3,2,0,1:T(8,128)(2,1)} %reshape.44, bf16[24,64,32]{2,1,0:T(8,128)(2,1)S(1)} %copy-done.1), kind=kOutput, calls=%fused_computation.17 | convolution fusion | flops 66404352 | bytes 2850816 | tf_op jit(solution)/shard_map/rac,rkad->rkcd/dot_general | solution.py:39
  230.0 2.2 copy.62
  233.4 1.2 fusion.25
  235.6 4.9 %scatter_fusion.1 = f32[24,7,1024]{2,1,0:T(8,128)} fusion(f32[24,7,1024]{2,1,0:T(8,128)} %broadcast_in_dim.16, s32[24]{0:T(128)} %copy-done.6, f32[24,7,1024]{2,1,0:T(8,128)S(1)} %fusion.25), kind=kCustom, calls=%fused_computation.5 | custom fusion | bytes 2064480 | tf_op jit(solution)/shard_map/scatter | solution.py:57
  240.5 4.1 %all-to-all-start.3 = ((f32[24,7,1024]{2,1,0:T(8,128)}), f32[24,7,1024]{2,1,0:T(8,128)S(1)}, u32[]{:S(2)}, u32[]{:S(2)}) async-start(f32[24,7,1024]{2,1,0:T(8,128)} %scatter_fusion.1), calls=%async_computation.3 | async-start | bytes 1572864 | tf_op jit(solution)/shard_map/all_to_all | solution.py:118
  244.6 12.6 %all-to-all-done.3 = f32[24,7,1024]{2,1,0:T(8,128)S(1)} async-done(((f32[24,7,1024]{2,1,0:T(8,128)}), f32[24,7,1024]{2,1,0:T(8,128)S(1)}, u32[]{:S(2)}, u32[]{:S(2)}) %all-to-all-start.3) | async-done | bytes 688160 | tf_op jit(solution)/shard_map/all_to_all | solution.py:118
  (55 shorter events, 16.2 us)
Async XLA Ops:
  7.2 22.0 %collective-permute-start = (bf16[48,8192]{1,0:T(8,128)(2,1)}, bf16[48,8192]{1,0:T(8,128)(2,1)S(1)}, u32[]{:S(2)}, u32[]{:S(2)}) collective-permute-start(bf16[48,8192]{1,0:T(8,128)(2,1)} %param.12), channel_id=1, source_target_pairs={{0,8},{8,16},{16,24},{1,9},{9,17},{17,25},{2,10},{10,18},{18,26},{... | collective-permute-start | bytes 2359304 | tf_op jit(solution)/shard_map/ppermute | solution.py:15
  12.2 21.2 %collective-permute-start.1 = (bf16[48,8192]{1,0:T(8,128)(2,1)}, bf16[48,8192]{1,0:T(8,128)(2,1)}, u32[]{:S(2)}, u32[]{:S(2)}) collective-permute-start(bf16[48,8192]{1,0:T(8,128)(2,1)} %param.12), channel_id=1, source_target_pairs={{8,0},{16,8},{24,16},{9,1},{17,9},{25,17},{10,2},{18,10},{26,18},{... | collective-permute-start | bytes 2359304 | tf_op jit(solution)/shard_map/ppermute | solution.py:17
  17.4 103.7 %all-to-all-start = ((f32[8,1,144]{2,1,0:T(1,128)}), f32[8,1,144]{2,1,0:T(1,128)S(1)}, u32[]{:S(2)}, u32[]{:S(2)}) async-start(f32[8,1,144]{2,1,0:T(1,128)} %reshape.114), calls=%async_computation | async-start | bytes 16384 | tf_op jit(solution)/shard_map/all_to_all | solution.py:101
  41.8 16.0 %copy-start = (bf16[48,128,64]{2,1,0:T(8,128)(2,1)S(1)}, bf16[48,128,64]{2,1,0:T(8,128)(2,1)}, u32[]{:S(2)}) copy-start(bf16[48,128,64]{2,1,0:T(8,128)(2,1)} %reshape.42) | copy-start | bytes 2359300
  121.0 5.0 %copy-start.2 = (bf16[24,2048]{1,0:T(8,128)(2,1)S(1)}, bf16[24,2048]{1,0:T(8,128)(2,1)}, u32[]{:S(2)}) copy-start(bf16[24,2048]{1,0:T(8,128)(2,1)} %param.17) | copy-start | bytes 294916
  121.0 16.8 %copy-start.3 = (s32[24,7]{0,1:T(8,128)S(1)}, s32[24,7]{0,1:T(8,128)}, u32[]{:S(2)}) copy-start(s32[24,7]{0,1:T(8,128)} %param.18) | copy-start | bytes 2020
  121.0 17.0 %copy-start.4 = (s32[24,7]{0,1:T(8,128)S(1)}, s32[24,7]{0,1:T(8,128)}, u32[]{:S(2)}) copy-start(s32[24,7]{0,1:T(8,128)} %param.19) | copy-start | bytes 2020
  121.0 17.7 %copy-start.5 = (s32[24,1]{0,1:T(1,128)S(1)}, s32[24,1]{0,1:T(1,128)}, u32[]{:S(2)}) copy-start(s32[24,1]{0,1:T(1,128)} %param.20) | copy-start | bytes 292
  121.0 18.0 %copy-start.7 = (s32[24]{0:T(128)S(1)}, s32[24]{0:T(128)}, u32[]{:S(2)}) copy-start(s32[24]{0:T(128)} %param.21) | copy-start | bytes 292
  121.0 85.9 %all-to-all-start.1 = ((f32[48,7,4096]{2,1,0:T(8,128)}), f32[48,7,4096]{2,1,0:T(8,128)}, u32[]{:S(2)}, u32[]{:S(2)}) async-start(f32[48,7,4096]{2,1,0:T(8,128)} %scatter_fusion), calls=%async_computation.1 | async-start | bytes 12582912 | tf_op jit(solution)/shard_map/all_to_all | solution.py:100
  125.9 64.2 %all-gather.2.cloned.1.call-start = ((), (), s32[]{:S(2)}) async-start(), calls=%async_computation.4 | async-start | bytes 2654208 | tf_op jit(solution)/shard_map/all_gather | solution.py:109
  126.0 6.0 %collective-permute-start.2 = (bf16[24,2048]{1,0:T(8,128)(2,1)S(1)}, bf16[24,2048]{1,0:T(8,128)(2,1)S(1)}, u32[]{:S(2)}, u32[]{:S(2)}) collective-permute-start(bf16[24,2048]{1,0:T(8,128)(2,1)S(1)} %copy-done.2), channel_id=1, source_target_pairs={{0,8},{8,16},{16,24},{1,9},{9,17},{17,25},{2,10},{10,18},{18,26},{... | collective-permute-start | bytes 294920 | tf_op jit(solution)/shard_map/ppermute | solution.py:15
  129.4 6.6 %collective-permute-start.3 = (bf16[24,2048]{1,0:T(8,128)(2,1)S(1)}, bf16[24,2048]{1,0:T(8,128)(2,1)S(1)}, u32[]{:S(2)}, u32[]{:S(2)}) collective-permute-start(bf16[24,2048]{1,0:T(8,128)(2,1)S(1)} %copy-done.2), channel_id=1, source_target_pairs={{8,0},{16,8},{24,16},{9,1},{17,9},{25,17},{10,2},{18,10},{26,18},{... | collective-permute-start | bytes 294920 | tf_op jit(solution)/shard_map/ppermute | solution.py:17
  139.1 1.9 copy-start.6
  207.0 33.5 %all-to-all-start.2 = ((f32[8,3,12]{2,1,0:T(4,128)}), f32[8,3,12]{2,1,0:T(4,128)S(1)}, u32[]{:S(2)}, u32[]{:S(2)}) async-start(f32[8,3,12]{2,1,0:T(4,128)} %all_to_all.26), calls=%async_computation.2 | async-start | bytes 32768 | tf_op jit(solution)/shard_map/all_to_all | solution.py:119
  210.3 14.4 %copy-start.1 = (bf16[24,64,32]{2,1,0:T(8,128)(2,1)S(1)}, bf16[24,64,32]{2,1,0:T(8,128)(2,1)}, u32[]{:S(2)}) copy-start(bf16[24,64,32]{2,1,0:T(8,128)(2,1)} %reshape.48) | copy-start | bytes 294916
  240.5 16.7 %all-to-all-start.3 = ((f32[24,7,1024]{2,1,0:T(8,128)}), f32[24,7,1024]{2,1,0:T(8,128)S(1)}, u32[]{:S(2)}, u32[]{:S(2)}) async-start(f32[24,7,1024]{2,1,0:T(8,128)} %scatter_fusion.1), calls=%async_computation.3 | async-start | bytes 1572864 | tf_op jit(solution)/shard_map/all_to_all | solution.py:118
Sparse Core Ops, SparseCore 0:
  137.0 53.0 all-gather.1
where the time goes:
time: 268 us; the launch traced here: 266 us
  local copies, waits for them, and re-layouts  90.1 us (34%)
  waiting for transfers between devices  84.4 us (31%)
  matrix products  41.8 us (16%)
  starting transfers between devices  27.3 us (10%)
  between operations  14.2 us (5%)
  other arithmetic  7.92 us (3%)
    all_gather x1, waiting for transfers between devices, local(): collected = lax.all_gather(stacked, 'dom', axis=1, tiled=True)  48.3 us
    reshape x4, local copies, waits for them, and re-layouts, restrict_terms(): term = term.reshape(count, stencil, narrow * narrow)  25.8 us
    dot_general x2, matrix products, restrict_terms(): jnp.einsum('rac,rkad->rkcd', own_rows, product, preferred_element_type=jn...  21.9 us
    scatter x2, local copies, waits for them, and re-layouts, place_into(): jnp.zeros((slots,) + values.shape[1:], values.dtype).at[position]  17.2 us
    reshape x1, local copies, waits for them, and re-layouts, local(): picked = nearby_rows[index].reshape(rows, stencil, width, narrow)  16 us
    all_to_all x1, waiting for transfers between devices, local(): lax.all_to_all(sent2, 'dom', split_axis=0, concat_axis=0, tiled=True)  12.6 us
    all_to_all x1, waiting for transfers between devices, local(): lax.all_to_all(sent, 'dom', split_axis=0, concat_axis=0, tiled=True)  11.2 us
    dot_general x2, matrix products, restrict_terms(): jnp.einsum('rks,rkx->rsx', choose, term, precision=lax.Precision.HIGHEST)  9.63 us
  transfers between devices with their start and end apart: 9, of which 7 were waited for; matrix products, arithmetic and copies ran while one was open for 52% of the time, Pallas kernels for 0%

commit v1 on v0

--- a/solution.py
+++ b/solution.py
@@ -1,7 +1,39 @@
+import functools
 import jax
 import jax.numpy as jnp
 from jax import lax
 from jax.sharding import PartitionSpec as P
+
+
+def panels_handle(vector, bus_axis):
+    built, upper, item_now = (lax.axis_size(bus_axis), lax.axis_index(bus_axis), vector.shape[1])
+    views = []
+    for u, kk in enumerate(vector.shape):
+        views.append(kk * built if u == 1 else kk)
+    last = lax.dynamic_update_slice_in_dim(
+        jnp.zeros(views, vector.dtype), vector, upper * item_now, axis=1
+    )
+    view_out = e_next = vector
+    for j in range(1, built // 2 + 1):
+        column = []
+        for u in range(built):
+            column.append((u, (u + 1) % built))
+        view_out = lax.ppermute(view_out, axis_name=bus_axis, perm=column)
+        last = lax.dynamic_update_slice_in_dim(
+            last, view_out, (upper - j) % built * item_now, axis=1
+        )
+        if 2 * j < built:
+            store = []
+            for u in range(built):
+                store.append((u, (u - 1) % built))
+            e_next = lax.ppermute(e_next, axis_name=bus_axis, perm=store)
+            last = lax.dynamic_update_slice_in_dim(
+                last, e_next, (upper + j) % built * item_now, axis=1
+            )
+    return last
+
+
+_get_zones = functools.partial(panels_handle, bus_axis="dom")
 
 
 def extended(cells, sides, width):
@@ -106,7 +138,7 @@
     flat = coarse_interp.shape[1]
     widened = extended(coarse_interp, (("region", 0),), owned)
     stacked = widened.reshape(3, owned, flat)
-    collected = lax.all_gather(stacked, "dom", axis=1, tiled=True)
+    collected = _get_zones(stacked)
     table = collected.reshape(3 * span2, flat)
     index2 = (coarse_cols // span2 - region + 1) * span2 + coarse_cols % span2
     picked2 = table[index2].reshape(owned, stencil, narrow, narrow2)

time: 268 us -> 281 us (1.049)
  waiting for transfers between devices: 84.4 us -> 105 us
  between operations: 14.2 us -> 1.08 us
  starting transfers between devices: 27.3 us -> 35.4 us
    ppermute x0 -> x7, waiting for transfers between devices: none -> 84.1 us  [the longest x4 84.1 us: panels_handle(): view_out = lax.ppermute(view_out, axis_name=bus_axis, perm=column)]
    all_gather x1 -> x0, waiting for transfers between devices: 48.3 us -> none  [local(): collected = lax.all_gather(stacked, 'dom', axis=1, tiled=True)]
    all_to_all x1, waiting for transfers between devices: 11.2 us -> 0.01 us  [local(): lax.all_to_all(sent, 'dom', split_axis=0, concat_axis=0, tiled=True)]
    ppermute x0 -> x7, starting transfers between devices: none -> 7.98 us  [the longest x3 7.92 us: panels_handle(): e_next = lax.ppermute(e_next, axis_name=bus_axis, perm=store)]
    ppermute x2, waiting for transfers between devices: 8.28 us -> 4.94 us  [extended(): lax.ppermute(head, axis, [((i + 1) % count, i) for i in range(ends)])]
  transfers between devices with their start and end apart: 9 -> 15, of which waited for: 7 -> 8; matrix products, arithmetic and copies ran while one was open for 52% -> 48% of each run, Pallas kernels for 0% -> 0%
where the time goes in v1:
time: 281 us; the launch traced here: 279 us
  waiting for transfers between devices  105 us (37%)
  local copies, waits for them, and re-layouts  88.8 us (32%)
  matrix products  41.8 us (15%)
  starting transfers between devices  35.4 us (13%)
  other arithmetic  7.17 us (3%)
    ppermute x4, waiting for transfers between devices, panels_handle(): view_out = lax.ppermute(view_out, axis_name=bus_axis, perm=column)  84.1 us
    reshape x4, local copies, waits for them, and re-layouts, restrict_terms(): term = term.reshape(count, stencil, narrow * narrow)  25.8 us
    dot_general x2, matrix products, restrict_terms(): jnp.einsum('rac,rkad->rkcd', own_rows, product, preferred_element_type=jn...  21.9 us
    scatter x2, local copies, waits for them, and re-layouts, place_into(): jnp.zeros((slots,) + values.shape[1:], values.dtype).at[position]  17.2 us
    reshape x1, local copies, waits for them, and re-layouts, local(): picked = nearby_rows[index].reshape(rows, stencil, width, narrow)  16 us
    all_to_all x1, waiting for transfers between devices, local(): lax.all_to_all(sent2, 'dom', split_axis=0, concat_axis=0, tiled=True)  12.6 us
    dot_general x2, matrix products, restrict_terms(): jnp.einsum('rks,rkx->rsx', choose, term, precision=lax.Precision.HIGHEST)  9.64 us
    dot_general x1, matrix products, local(): jnp.einsum('rc,rkx->ckx', labels, arrived, precision=lax.Precision.HIGHEST)  9.33 us
  transfers between devices with their start and end apart: 15, of which 8 were waited for; matrix products, arithmetic and copies ran while one was open for 48% of the time, Pallas kernels for 0%

profile of v1, /device:TPU:0, one launch (start us, length us, event | category | flops | bytes accessed | tf_op | source)
XLA Modules:
  0.0 278.9 jit_solution(10495383827097356005)
XLA Ops:
  0.6 5.1 %collective-permute-start = (bf16[48,8192]{1,0:T(8,128)(2,1)}, bf16[48,8192]{1,0:T(8,128)(2,1)S(1)}, u32[]{:S(2)}, u32[]{:S(2)}) collective-permute-start(bf16[48,8192]{1,0:T(8,128)(2,1)} %param.12), channel_id=1, source_target_pairs={{0,8},{8,16},{16,24},{1,9},{9,17},{17,25},{2,10},{10,18},{18,26},{... | collective-permute-start | bytes 2359304 | tf_op jit(solution)/shard_map/ppermute | solution.py:47
  11.0 3.7 %all-to-all-start = ((f32[8,1,144]{2,1,0:T(1,128)}), f32[8,1,144]{2,1,0:T(1,128)S(1)}, u32[]{:S(2)}, u32[]{:S(2)}) async-start(f32[8,1,144]{2,1,0:T(1,128)} %reshape.114), calls=%async_computation | async-start | bytes 16384 | tf_op jit(solution)/shard_map/all_to_all | solution.py:133
  14.7 3.4 %reshape.42 = bf16[48,128,64]{2,1,0:T(8,128)(2,1)} reshape(bf16[48,8192]{1,0:T(8,128)(2,1)} %param.12) | data formatting | bytes 1572864 | tf_op jit(solution)/shard_map/reshape | solution.py:128
  19.8 3.0 %collective-permute-done = bf16[48,8192]{1,0:T(8,128)(2,1)S(1)} collective-permute-done((bf16[48,8192]{1,0:T(8,128)(2,1)}, bf16[48,8192]{1,0:T(8,128)(2,1)S(1)}, u32[]{:S(2)}, u32[]{:S(2)}) %collective-permute-start) | collective-permute-done | bytes 786464 | tf_op jit(solution)/shard_map/ppermute | solution.py:47
  23.7 3.3 %collective-permute-done.1 = bf16[48,8192]{1,0:T(8,128)(2,1)} collective-permute-done((bf16[48,8192]{1,0:T(8,128)(2,1)}, bf16[48,8192]{1,0:T(8,128)(2,1)}, u32[]{:S(2)}, u32[]{:S(2)}) %collective-permute-start.1) | collective-permute-done | bytes 786464 | tf_op jit(solution)/shard_map/ppermute | solution.py:49
  28.5 6.9 %gather_fusion = bf16[336,8192]{1,0:T(8,128)(2,1)} fusion(bf16[144,8192]{1,0:T(8,128)(2,1)S(1)} %pad_maximum_fusion, s32[1024]{0:T(1024)S(1)} %pad_clamp_fusion.1), kind=kCustom, calls=%fused_computation | custom fusion | bytes 11011392 | tf_op jit(solution)/shard_map/gather | solution.py:127
  35.4 16.0 %reshape.41 = bf16[48,7,128,64]{3,2,1,0:T(8,128)(2,1)} reshape(bf16[336,8192]{1,0:T(8,128)(2,1)} %gather_fusion) | data formatting | bytes 11010048 | tf_op jit(solution)/shard_map/reshape | solution.py:127
  51.5 16.5 %fusion.10 = f32[48,7,64,64]{2,3,1,0:T(8,128)} fusion(bf16[48,7,128,64]{3,2,1,0:T(8,128)(2,1)} %reshape.41, bf16[48,7,128,128]{3,2,1,0:T(8,128)(2,1)} %param.11, bf16[48,128,64]{2,1,0:T(8,128)(2,1)S(1)} %copy-done), kind=kOutput, calls=%fused_computation.13 | convolution fusion | flops 1059717120 | bytes 22806528 | tf_op jit(solution)/shard_map/rac,rkad->rkcd/dot_general | solution.py:71
  68.0 12.2 %copy.58 = f32[48,7,64,64]{3,2,1,0:T(8,128)} copy(f32[48,7,64,64]{2,3,1,0:T(8,128)} %fusion.10) | data formatting | bytes 11010048 | tf_op jit(solution)/shard_map/reshape | solution.py:72
  80.2 10.3 %reshape.108 = f32[48,7,4096]{2,1,0:T(8,128)} reshape(f32[48,7,64,64]{3,2,1,0:T(8,128)} %copy.58) | data formatting | bytes 11010048 | tf_op jit(solution)/shard_map/reshape | solution.py:72
  90.4 8.4 %fusion.23 = f32[48,7,4096]{2,1,0:T(8,128)} fusion(f32[48,7,4096]{2,1,0:T(8,128)} %reshape.108, s32[48,7]{1,0:T(8,128)S(1)} %copy.31), kind=kOutput, calls=%fused_computation.25 | convolution fusion | flops 115607856 | bytes 11011392 | tf_op jit(solution)/shard_map/rks,rkx->rsx/dot_general | solution.py:73
  98.9 3.4 %broadcast_in_dim.15 = f32[48,7,4096]{2,1,0:T(8,128)} broadcast(f32[]{:T(128)} %constant.110.clone.1), dimensions={} | broadcast | bytes 5505028 | tf_op jit(solution)/shard_map/broadcast_in_dim | solution.py:89
  102.3 12.2 %scatter_fusion = f32[48,7,4096]{2,1,0:T(8,128)} fusion(f32[48,7,4096]{2,1,0:T(8,128)} %broadcast_in_dim.15, s32[48]{0:T(128)S(1)} %fusion.49, f32[48,7,4096]{2,1,0:T(8,128)} %fusion.23), kind=kCustom, calls=%fused_computation.3 | custom fusion | bytes 16515264 | tf_op jit(solution)/shard_map/scatter | solution.py:89
  114.5 5.1 %all-to-all-start.1 = ((f32[48,7,4096]{2,1,0:T(8,128)}), f32[48,7,4096]{2,1,0:T(8,128)}, u32[]{:S(2)}, u32[]{:S(2)}) async-start(f32[48,7,4096]{2,1,0:T(8,128)} %scatter_fusion), calls=%async_computation.1 | async-start | bytes 12582912 | tf_op jit(solution)/shard_map/all_to_all | solution.py:132
  119.6 3.5 %collective-permute-start.2 = (bf16[24,2048]{1,0:T(8,128)(2,1)S(1)}, bf16[24,2048]{1,0:T(8,128)(2,1)S(1)}, u32[]{:S(2)}, u32[]{:S(2)}) collective-permute-start(bf16[24,2048]{1,0:T(8,128)(2,1)S(1)} %copy-done.4), channel_id=1, source_target_pairs={{0,8},{8,16},{16,24},{1,9},{9,17},{17,25},{2,10},{10,18},{18,26},{... | collective-permute-start | bytes 294920 | tf_op jit(solution)/shard_map/ppermute | solution.py:47
  128.1 1.6 collective-permute-done.3
  129.9 2.6 collective-permute-start.5
  134.1 62.8 %collective-permute-done.4 = bf16[3,24,2048]{2,1,0:T(8,128)(2,1)S(1)} collective-permute-done((bf16[3,24,2048]{2,1,0:T(8,128)(2,1)S(1)}, bf16[3,24,2048]{2,1,0:T(8,128)(2,1)S(1)}, u32[]{:S(2)}, u32[]{:S(2)}) %collective-permute-start.4) | collective-permute-done | bytes 294944 | tf_op jit(solution)/shard_map/ppermute | solution.py:21
  197.0 2.6 collective-permute-start.7
  199.7 7.5 %collective-permute-done.6 = bf16[3,24,2048]{2,1,0:T(8,128)(2,1)S(1)} collective-permute-done((bf16[3,24,2048]{2,1,0:T(8,128)(2,1)S(1)}, bf16[3,24,2048]{2,1,0:T(8,128)(2,1)S(1)}, u32[]{:S(2)}, u32[]{:S(2)}) %collective-permute-start.6) | collective-permute-done | bytes 294944 | tf_op jit(solution)/shard_map/ppermute | solution.py:21
  207.2 2.6 collective-permute-start.9
  209.9 6.8 %collective-permute-done.8 = bf16[3,24,2048]{2,1,0:T(8,128)(2,1)S(1)} collective-permute-done((bf16[3,24,2048]{2,1,0:T(8,128)(2,1)S(1)}, bf16[3,24,2048]{2,1,0:T(8,128)(2,1)S(1)}, u32[]{:S(2)}, u32[]{:S(2)}) %collective-permute-start.8) | collective-permute-done | bytes 294944 | tf_op jit(solution)/shard_map/ppermute | solution.py:21
  216.8 7.0 %collective-permute-done.10 = bf16[3,24,2048]{2,1,0:T(8,128)(2,1)S(1)} collective-permute-done((bf16[3,24,2048]{2,1,0:T(8,128)(2,1)S(1)}, bf16[3,24,2048]{2,1,0:T(8,128)(2,1)S(1)}, u32[]{:S(2)}, u32[]{:S(2)}) %collective-permute-start.10) | collective-permute-done | bytes 294944 | tf_op jit(solution)/shard_map/ppermute | solution.py:21
  224.9 2.0 reshape.47
  226.9 3.3 %all-to-all-start.2 = ((f32[8,3,12]{2,1,0:T(4,128)}), f32[8,3,12]{2,1,0:T(4,128)S(1)}, u32[]{:S(2)}, u32[]{:S(2)}) async-start(f32[8,3,12]{2,1,0:T(4,128)} %all_to_all.26), calls=%async_computation.2 | async-start | bytes 32768 | tf_op jit(solution)/shard_map/all_to_all | solution.py:151
  230.2 9.3 %fusion.7 = bf16[24,7,4096]{2,0,1:T(8,128)(2,1)} fusion(f32[48,7,4096]{2,1,0:T(8,128)} %all-to-all-done.1, f32[48,24]{1,0:T(8,128)S(1)} %all_to_all.24), kind=kOutput, calls=%fused_computation.12 | convolution fusion | flops 397049856 | bytes 6885888 | tf_op jit(solution)/shard_map/rc,rkx->ckx/dot_general | solution.py:135
  239.6 5.0 %reshape.44 = bf16[24,7,64,64]{3,2,0,1:T(8,128)(2,1)} reshape(bf16[24,7,4096]{2,0,1:T(8,128)(2,1)} %fusion.7) | data formatting | bytes 2752512 | tf_op jit(solution)/shard_map/reshape | solution.py:145
  244.6 5.3 %convolution_bitcast_fusion = f32[24,7,32,32]{2,3,1,0:T(8,128)} fusion(bf16[24,7,64,32]{3,2,1,0:T(8,128)(2,1)S(1)} %reshape.47, bf16[24,7,64,64]{3,2,0,1:T(8,128)(2,1)} %reshape.44, bf16[24,64,32]{2,1,0:T(8,128)(2,1)S(1)} %copy-done.2), kind=kOutput, calls=%fused_computation.17 | convolution fusion | flops 66404352 | bytes 2850816 | tf_op jit(solution)/shard_map/rac,rkad->rkcd/dot_general | solution.py:71
  249.9 2.2 copy.62
  255.5 5.0 %scatter_fusion.1 = f32[24,7,1024]{2,1,0:T(8,128)} fusion(f32[24,7,1024]{2,1,0:T(8,128)} %broadcast_in_dim.18, s32[24]{0:T(128)} %copy-done.8, f32[24,7,1024]{2,1,0:T(8,128)S(1)} %fusion.25), kind=kCustom, calls=%fused_computation.5 | custom fusion | bytes 2064480 | tf_op jit(solution)/shard_map/scatter | solution.py:89
  260.5 4.1 %all-to-all-start.3 = ((f32[24,7,1024]{2,1,0:T(8,128)}), f32[24,7,1024]{2,1,0:T(8,128)S(1)}, u32[]{:S(2)}, u32[]{:S(2)}) async-start(f32[24,7,1024]{2,1,0:T(8,128)} %scatter_fusion.1), calls=%async_computation.3 | async-start | bytes 1572864 | tf_op jit(solution)/shard_map/all_to_all | solution.py:150
  264.6 12.6 %all-to-all-done.3 = f32[24,7,1024]{2,1,0:T(8,128)S(1)} async-done(((f32[24,7,1024]{2,1,0:T(8,128)}), f32[24,7,1024]{2,1,0:T(8,128)S(1)}, u32[]{:S(2)}, u32[]{:S(2)}) %all-to-all-start.3) | async-done | bytes 688160 | tf_op jit(solution)/shard_map/all_to_all | solution.py:150
  (79 shorter events, 22.1 us)
Async XLA Ops:
  0.6 26.3 %copy-start.1 = (bf16[48,8192]{1,0:T(8,128)(2,1)S(1)}, bf16[48,8192]{1,0:T(8,128)(2,1)}, u32[]{:S(2)}) copy-start(bf16[48,8192]{1,0:T(8,128)(2,1)} %param.12) | copy-start | bytes 2359300
  0.6 22.2 %collective-permute-start = (bf16[48,8192]{1,0:T(8,128)(2,1)}, bf16[48,8192]{1,0:T(8,128)(2,1)S(1)}, u32[]{:S(2)}, u32[]{:S(2)}) collective-permute-start(bf16[48,8192]{1,0:T(8,128)(2,1)} %param.12), channel_id=1, source_target_pairs={{0,8},{8,16},{16,24},{1,9},{9,17},{17,25},{2,10},{10,18},{18,26},{... | collective-permute-start | bytes 2359304 | tf_op jit(solution)/shard_map/ppermute | solution.py:47
  5.8 21.2 %collective-permute-start.1 = (bf16[48,8192]{1,0:T(8,128)(2,1)}, bf16[48,8192]{1,0:T(8,128)(2,1)}, u32[]{:S(2)}, u32[]{:S(2)}) collective-permute-start(bf16[48,8192]{1,0:T(8,128)(2,1)} %param.12), channel_id=1, source_target_pairs={{8,0},{16,8},{24,16},{9,1},{17,9},{25,17},{10,2},{18,10},{26,18},{... | collective-permute-start | bytes 2359304 | tf_op jit(solution)/shard_map/ppermute | solution.py:49
  11.0 103.5 %all-to-all-start = ((f32[8,1,144]{2,1,0:T(1,128)}), f32[8,1,144]{2,1,0:T(1,128)S(1)}, u32[]{:S(2)}, u32[]{:S(2)}) async-start(f32[8,1,144]{2,1,0:T(1,128)} %reshape.114), calls=%async_computation | async-start | bytes 16384 | tf_op jit(solution)/shard_map/all_to_all | solution.py:133
  22.8 0.9 copy-start.3
  35.4 16.0 %copy-start = (bf16[48,128,64]{2,1,0:T(8,128)(2,1)S(1)}, bf16[48,128,64]{2,1,0:T(8,128)(2,1)}, u32[]{:S(2)}) copy-start(bf16[48,128,64]{2,1,0:T(8,128)(2,1)} %reshape.42) | copy-start | bytes 2359300
  114.5 5.1 %copy-start.4 = (bf16[24,2048]{1,0:T(8,128)(2,1)S(1)}, bf16[24,2048]{1,0:T(8,128)(2,1)}, u32[]{:S(2)}) copy-start(bf16[24,2048]{1,0:T(8,128)(2,1)} %param.17) | copy-start | bytes 294916
  114.5 9.9 %copy-start.7 = (s32[24,1]{0,1:T(1,128)S(1)}, s32[24,1]{0,1:T(1,128)}, u32[]{:S(2)}) copy-start(s32[24,1]{0,1:T(1,128)} %param.20) | copy-start | bytes 292
  114.5 10.2 %copy-start.5 = (s32[24,7]{0,1:T(8,128)S(1)}, s32[24,7]{0,1:T(8,128)}, u32[]{:S(2)}) copy-start(s32[24,7]{0,1:T(8,128)} %param.18) | copy-start | bytes 2020
  114.5 11.6 %copy-start.6 = (s32[24,7]{0,1:T(8,128)S(1)}, s32[24,7]{0,1:T(8,128)}, u32[]{:S(2)}) copy-start(s32[24,7]{0,1:T(8,128)} %param.19) | copy-start | bytes 2020
  114.5 12.3 %copy-start.9 = (s32[24]{0:T(128)S(1)}, s32[24]{0:T(128)}, u32[]{:S(2)}) copy-start(s32[24]{0:T(128)} %param.21) | copy-start | bytes 292
  114.5 112.3 %all-to-all-start.1 = ((f32[48,7,4096]{2,1,0:T(8,128)}), f32[48,7,4096]{2,1,0:T(8,128)}, u32[]{:S(2)}, u32[]{:S(2)}) async-start(f32[48,7,4096]{2,1,0:T(8,128)} %scatter_fusion), calls=%async_computation.1 | async-start | bytes 12582912 | tf_op jit(solution)/shard_map/all_to_all | solution.py:132
  119.6 8.5 %collective-permute-start.2 = (bf16[24,2048]{1,0:T(8,128)(2,1)S(1)}, bf16[24,2048]{1,0:T(8,128)(2,1)S(1)}, u32[]{:S(2)}, u32[]{:S(2)}) collective-permute-start(bf16[24,2048]{1,0:T(8,128)(2,1)S(1)} %copy-done.4), channel_id=1, source_target_pairs={{0,8},{8,16},{16,24},{1,9},{9,17},{17,25},{2,10},{10,18},{18,26},{... | collective-permute-start | bytes 294920 | tf_op jit(solution)/shard_map/ppermute | solution.py:47
  123.1 6.7 %collective-permute-start.3 = (bf16[24,2048]{1,0:T(8,128)(2,1)S(1)}, bf16[24,2048]{1,0:T(8,128)(2,1)S(1)}, u32[]{:S(2)}, u32[]{:S(2)}) collective-permute-start(bf16[24,2048]{1,0:T(8,128)(2,1)S(1)} %copy-done.4), channel_id=1, source_target_pairs={{8,0},{16,8},{24,16},{9,1},{17,9},{25,17},{10,2},{18,10},{26,18},{... | collective-permute-start | bytes 294920 | tf_op jit(solution)/shard_map/ppermute | solution.py:49
  124.8 7.7 %copy-start.8 = (s32[24]{0:T(128)}, s32[24]{0:T(128)S(1)}, u32[]{:S(2)}) copy-start(s32[24]{0:T(128)S(1)} %fusion.50) | copy-start | bytes 292
  129.8 67.1 %collective-permute-start.4 = (bf16[3,24,2048]{2,1,0:T(8,128)(2,1)S(1)}, bf16[3,24,2048]{2,1,0:T(8,128)(2,1)S(1)}, u32[]{:S(2)}, u32[]{:S(2)}) collective-permute-start(bf16[3,24,2048]{2,1,0:T(8,128)(2,1)S(1)} %bitcast.53), channel_id=1, source_target_pairs={{0,1},{1,2},{2,3},{3,4},{4,5},{5,6},{6,7},{7,0},{8,9},{9,10},{10,1... | collective-permute-start | bytes 884744 | tf_op jit(solution)/shard_map/ppermute | solution.py:21
  129.9 67.1 %collective-permute-start.5 = (bf16[3,24,2048]{2,1,0:T(8,128)(2,1)S(1)}, bf16[3,24,2048]{2,1,0:T(8,128)(2,1)S(1)}, u32[]{:S(2)}, u32[]{:S(2)}) collective-permute-start(bf16[3,24,2048]{2,1,0:T(8,128)(2,1)S(1)} %bitcast.54), channel_id=1, source_target_pairs={{0,7},{1,0},{2,1},{3,2},{4,3},{5,4},{6,5},{7,6},{8,15},{9,8},{10,9... | collective-permute-start | bytes 884744 | tf_op jit(solution)/shard_map/ppermute | solution.py:29
  197.0 10.2 %collective-permute-start.6 = (bf16[3,24,2048]{2,1,0:T(8,128)(2,1)S(1)}, bf16[3,24,2048]{2,1,0:T(8,128)(2,1)S(1)}, u32[]{:S(2)}, u32[]{:S(2)}) collective-permute-start(bf16[3,24,2048]{2,1,0:T(8,128)(2,1)S(1)} %collective-permute-done.4), channel_id=1, source_target_pairs={{0,1},{1,2},{2,3},{3,4},{4,5},{5,6},{6,7},{7,0},{8,9},{9,10},{10,1... | collective-permute-start | bytes 884744 | tf_op jit(solution)/shard_map/ppermute | solution.py:21
  197.0 10.2 %collective-permute-start.7 = (bf16[3,24,2048]{2,1,0:T(8,128)(2,1)S(1)}, bf16[3,24,2048]{2,1,0:T(8,128)(2,1)S(1)}, u32[]{:S(2)}, u32[]{:S(2)}) collective-permute-start(bf16[3,24,2048]{2,1,0:T(8,128)(2,1)S(1)} %collective-permute-done.5), channel_id=1, source_target_pairs={{0,7},{1,0},{2,1},{3,2},{4,3},{5,4},{6,5},{7,6},{8,15},{9,8},{10,9... | collective-permute-start | bytes 884744 | tf_op jit(solution)/shard_map/ppermute | solution.py:29
  207.1 9.5 %collective-permute-start.8 = (bf16[3,24,2048]{2,1,0:T(8,128)(2,1)S(1)}, bf16[3,24,2048]{2,1,0:T(8,128)(2,1)S(1)}, u32[]{:S(2)}, u32[]{:S(2)}) collective-permute-start(bf16[3,24,2048]{2,1,0:T(8,128)(2,1)S(1)} %collective-permute-done.6), channel_id=1, source_target_pairs={{0,1},{1,2},{2,3},{3,4},{4,5},{5,6},{6,7},{7,0},{8,9},{9,10},{10,1... | collective-permute-start | bytes 884744 | tf_op jit(solution)/shard_map/ppermute | solution.py:21
  207.2 9.6 %collective-permute-start.9 = (bf16[3,24,2048]{2,1,0:T(8,128)(2,1)S(1)}, bf16[3,24,2048]{2,1,0:T(8,128)(2,1)S(1)}, u32[]{:S(2)}, u32[]{:S(2)}) collective-permute-start(bf16[3,24,2048]{2,1,0:T(8,128)(2,1)S(1)} %collective-permute-done.7), channel_id=1, source_target_pairs={{0,7},{1,0},{2,1},{3,2},{4,3},{5,4},{6,5},{7,6},{8,15},{9,8},{10,9... | collective-permute-start | bytes 884744 | tf_op jit(solution)/shard_map/ppermute | solution.py:29
  216.7 7.0 %collective-permute-start.10 = (bf16[3,24,2048]{2,1,0:T(8,128)(2,1)S(1)}, bf16[3,24,2048]{2,1,0:T(8,128)(2,1)S(1)}, u32[]{:S(2)}, u32[]{:S(2)}) collective-permute-start(bf16[3,24,2048]{2,1,0:T(8,128)(2,1)S(1)} %collective-permute-done.8), channel_id=1, source_target_pairs={{0,1},{1,2},{2,3},{3,4},{4,5},{5,6},{6,7},{7,0},{8,9},{9,10},{10,1... | collective-permute-start | bytes 884744 | tf_op jit(solution)/shard_map/ppermute | solution.py:21
  226.9 33.6 %all-to-all-start.2 = ((f32[8,3,12]{2,1,0:T(4,128)}), f32[8,3,12]{2,1,0:T(4,128)S(1)}, u32[]{:S(2)}, u32[]{:S(2)}) async-start(f32[8,3,12]{2,1,0:T(4,128)} %all_to_all.26), calls=%async_computation.2 | async-start | bytes 32768 | tf_op jit(solution)/shard_map/all_to_all | solution.py:151
  239.6 5.0 %copy-start.2 = (bf16[24,64,32]{2,1,0:T(8,128)(2,1)S(1)}, bf16[24,64,32]{2,1,0:T(8,128)(2,1)}, u32[]{:S(2)}) copy-start(bf16[24,64,32]{2,1,0:T(8,128)(2,1)} %reshape.48) | copy-start | bytes 294916
  260.5 16.7 %all-to-all-start.3 = ((f32[24,7,1024]{2,1,0:T(8,128)}), f32[24,7,1024]{2,1,0:T(8,128)S(1)}, u32[]{:S(2)}, u32[]{:S(2)}) async-start(f32[24,7,1024]{2,1,0:T(8,128)} %scatter_fusion.1), calls=%async_computation.3 | async-start | bytes 1572864 | tf_op jit(solution)/shard_map/all_to_all | solution.py:150
